TPU v7x, 32 devices: a whole 2x2x4 slice. The times are simulated.
32 devices in a mesh: gx: 4 (over y, core), gy: 8 (over z, x).
Axes of the slice: x: 2, y: 2, z: 4, core: 2. Of those that a mesh axis runs over, the one named last changes fastest.
Arguments:
- a_rows: bfloat16 [196608, 1024], P(('gx', 'gy')), may hold values from -6 to 6
- heights: int32 [32], P('gx'), may hold values from 1 to 38, as said below
- destination: int32 [32, 48], P('gx'), may hold values from 0 to 1023, as said below
Outputs:
- ortho_rows: bfloat16 [131072, 1024], P(('gx', 'gy'))
- factor_r: float32 [1024, 1024], replicated
Inputs may be any that keep to these rules, and one draw needn't show every extreme that they name: Tiles 0 to heights[d] - 1 of device d are live, the others carry nothing of the problem; the largest value is reached in every draw. For a live tile, destination // 32 is a device with the same gx index as the tile's device; live tiles name distinct slots; one device sends at most one live tile to any other device; entries of tiles that are not live are meaningless.
All inputs are finite; a program needn't handle non-finite values.
Results may differ from a plain program's by a relative error of at most 0.00055.
Values may be sent and summed in bfloat16 or wider, within the bound.
A program may use at most 256 MiB of HBM per device.

v0:
```python
import math

import jax
import jax.numpy as jnp
from jax import lax
from jax.sharding import PartitionSpec as P

TILE = 128
SLOTS = 32


def factor(row_block):
    gram_local = lax.dot_general(
        row_block, row_block, (((0,), (0,)), ((), ())), preferred_element_type=jnp.float32
    )
    summed = lax.psum(gram_local, ("gx", "gy"))
    return jnp.linalg.cholesky(summed)


def normalise(low_factor, row_block, root_scale):
    solved = jax.scipy.linalg.solve_triangular(
        low_factor, row_block.astype(jnp.float32).T, lower=True
    )
    return (solved.T * root_scale).astype(jnp.bfloat16)


def on_device(a_rows, heights, destination):
    breadth = a_rows.shape[1]
    size_gy = lax.axis_size("gy")
    devices = lax.axis_size("gx") * size_gy
    group_pos = lax.axis_index("gy")
    my_index = lax.axis_index("gx") * size_gy + group_pos
    group_base = my_index - group_pos
    tile_stack = a_rows.reshape(-1, TILE, breadth)
    stored = tile_stack.shape[0]
    tile_ids = jnp.arange(stored, dtype=jnp.int32)
    peer_ids = jnp.arange(size_gy, dtype=jnp.int32)
    slot_ids = jnp.arange(SLOTS, dtype=jnp.int32)
    tile_live = tile_ids[None, :] < heights[:, None]
    target_dev = destination // SLOTS
    target_slot = destination % SLOTS
    own_live = tile_live[group_pos]
    own_dev = target_dev[group_pos]
    own_slot = target_slot[group_pos]
    leaving = own_live & (own_dev != my_index)
    chosen = leaving[None, :] & (own_dev[None, :] - group_base == peer_ids[:, None])
    send_index = jnp.sum(jnp.where(chosen, tile_ids[None, :], 0), axis=1)
    send_has = jnp.any(chosen, axis=1)
    arriving = tile_live & (target_dev == my_index) & (peer_ids[:, None] != group_pos)
    arrive_slot = jnp.sum(jnp.where(arriving, target_slot, 0), axis=1)
    arrive_has = jnp.any(arriving, axis=1)
    staying = own_live & (own_dev == my_index)
    own_match = staying[None, :] & (own_slot[None, :] == slot_ids[:, None])
    in_match = arrive_has[None, :] & (arrive_slot[None, :] == slot_ids[:, None])
    matched = jnp.concatenate([own_match, in_match], axis=1)
    source = jnp.sum(
        jnp.where(matched, jnp.arange(stored + size_gy, dtype=jnp.int32)[None, :], 0), axis=1
    )
    filled = jnp.any(matched, axis=1)
    root_scale = math.sqrt(devices * SLOTS * TILE)
    received = lax.all_to_all(
        jnp.where(send_has[:, None, None], tile_stack[send_index], jnp.zeros((), tile_stack.dtype)),
        "gy",
        split_axis=0,
        concat_axis=0,
        tiled=True,
    )
    combined = jnp.concatenate([tile_stack, received], axis=0)
    balanced = jnp.where(
        filled[:, None, None], combined[source], jnp.zeros((), tile_stack.dtype)
    ).reshape(-1, breadth)
    low_factor = factor(balanced)
    ortho_rows = normalise(low_factor, balanced, root_scale)
    return (ortho_rows, low_factor.T / root_scale)


def solution(mesh):
    placed = (P(("gx", "gy"), None), P("gx"), P("gx", None))
    return jax.shard_map(
        on_device,
        mesh=mesh,
        in_specs=placed,
        out_specs=(P(("gx", "gy"), None), P()),
        check_vma=False,
    )
```

profile of v0, /device:TPU:0, one launch (start us, length us, event | category | flops | bytes accessed | tf_op | source)
XLA Modules:
  0.0 704.3 jit_solution(5128577823372429109)
XLA Ops:
  16.0 7.3 %all-to-all-start = ((bf16[8,128,1024]{2,1,0:T(8,128)(2,1)}), bf16[8,128,1024]{2,1,0:T(8,128)(2,1)S(1)}, u32[]{:S(2)}, u32[]{:S(2)}) async-start(bf16[8,128,1024]{2,1,0:T(8,128)(2,1)} %broadcast_select_fusion), calls=%async_computation | async-start | bytes 4194304 | tf_op jit(solution)/shard_map/all_to_all | solution.py:61
  23.8 47.7 %all-to-all-done = bf16[8,128,1024]{2,1,0:T(8,128)(2,1)S(1)} async-done(((bf16[8,128,1024]{2,1,0:T(8,128)(2,1)}), bf16[8,128,1024]{2,1,0:T(8,128)(2,1)S(1)}, u32[]{:S(2)}, u32[]{:S(2)}) %all-to-all-start) | async-done | bytes 2097184 | tf_op jit(solution)/shard_map/all_to_all | solution.py:61
  71.5 13.6 %pad_maximum_fusion = bf16[56,128,1024]{2,1,0:T(8,128)(2,1)} fusion(bf16[8,128,1024]{2,1,0:T(8,128)(2,1)S(1)} %all-to-all-done, bf16[48,128,1024]{2,1,0:T(8,128)(2,1)} %bitcast.134), kind=kLoop, calls=%fused_computation.5 | loop fusion | flops 7340032 | bytes 29360128 | tf_op jit(solution)/shard_map/concatenate | solution.py:68
  85.1 10.2 %gather_fusion.1 = bf16[32,128,1024]{2,1,0:T(8,128)(2,1)} fusion(bf16[56,128,1024]{2,1,0:T(8,128)(2,1)} %pad_maximum_fusion, s32[1024]{0:T(1024)S(1)} %pad_clamp_fusion), kind=kCustom, calls=%fused_computation.1 | custom fusion | bytes 16777344 | tf_op jit(solution)/shard_map/gather | solution.py:70
  95.3 15.6 %fusion.30 = f32[1024,1024]{0,1:T(8,128)} fusion(bf16[32,128,1024]{2,1,0:T(8,128)(2,1)} %gather_fusion.1, pred[32]{0:T(512)(128)(4,1)S(1)} %reduce_or.41), kind=kOutput, calls=%fused_computation.43 | convolution fusion | flops 8594128896 | bytes 12582944 | tf_op jit(solution)/shard_map/dot_general | solution.py:13
  111.0 11.4 %copy.26 = bf16[4096,1024]{0,1:T(8,128)(2,1)} copy(bf16[4096,1024]{1,0:T(8,128)(2,1)} %bitcast.132) | data formatting | bytes 16777216 | tf_op jit(solution)/shard_map/gather | solution.py:70
  122.5 11.6 %fusion.90 = (f32[1024,4096]{1,0:T(8,128)}, bf16[1024,4096]{1,0:T(8,128)(2,1)}) fusion(bf16[4096,1024]{0,1:T(8,128)(2,1)} %copy.26, pred[4096]{0:T(1024)(128)(4,1)S(1)} %broadcast_bitcast_fusion), kind=kLoop, calls=%fused_computation.208 | loop fusion | flops 8388608 | bytes 33558528 | tf_op jit(solution)/shard_map/transpose | solution.py:22
  134.1 118.6 %all-reduce.3.cloned.1.call-done = f32[1024,1024]{0,1:T(8,128)} async-done(((f32[1024,1024]{0,1:T(8,128)}), f32[1024,1024]{0,1:T(8,128)}) %all-reduce.3.cloned.1.call-update) | async-done | bytes 4194320 | tf_op jit(solution)/shard_map/psum | solution.py:16
  264.7 11.7 %cholesky.223 = f32[128,128]{1,0:T(8,128)S(1)} custom-call(f32[128,128]{1,0:T(8,128)S(1)} %cholesky.580), custom_call_target="Cholesky" | custom-call | tf_op jit(solution)/shard_map/jit(cholesky)/cholesky | solution.py:17
  277.1 9.8 %custom-call.63 = f32[1,128,128]{1,2,0:T(8,128)S(1)} custom-call(f32[1,128,128]{2,1,0:T(8,128)S(1)} %get-tuple-element.83), custom_call_target="InvertDiagBlocksLowerTriangular" | custom-call | tf_op jit(solution)/shard_map/jit(cholesky)/cholesky | solution.py:17
  293.3 12.2 %cholesky.244 = f32[128,128]{1,0:T(8,128)S(1)} custom-call(f32[128,128]{1,0:T(8,128)S(1)} %cholesky.584), custom_call_target="Cholesky" | custom-call | tf_op jit(solution)/shard_map/jit(cholesky)/cholesky | solution.py:17
  306.8 9.8 %custom-call.64 = f32[1,128,128]{1,2,0:T(8,128)S(1)} custom-call(f32[1,128,128]{2,1,0:T(8,128)S(1)} %get-tuple-element.80), custom_call_target="InvertDiagBlocksLowerTriangular" | custom-call | tf_op jit(solution)/shard_map/jit(cholesky)/cholesky | solution.py:17
  319.9 11.7 %cholesky.468 = f32[128,128]{1,0:T(8,128)S(1)} custom-call(f32[128,128]{1,0:T(8,128)S(1)} %cholesky.589), custom_call_target="Cholesky" | custom-call | tf_op jit(solution)/shard_map/jit(cholesky)/cholesky | solution.py:17
  332.9 9.8 %custom-call.65 = f32[1,128,128]{1,2,0:T(8,128)S(1)} custom-call(f32[1,128,128]{2,1,0:T(8,128)S(1)} %get-tuple-element.77), custom_call_target="InvertDiagBlocksLowerTriangular" | custom-call | tf_op jit(solution)/shard_map/jit(cholesky)/cholesky | solution.py:17
  346.2 11.8 %cholesky.487 = f32[128,128]{1,0:T(8,128)S(1)} custom-call(f32[128,128]{1,0:T(8,128)S(1)} %cholesky.594), custom_call_target="Cholesky" | custom-call | tf_op jit(solution)/shard_map/jit(cholesky)/cholesky | solution.py:17
  359.4 9.8 %custom-call.66 = f32[1,128,128]{1,2,0:T(8,128)S(1)} custom-call(f32[1,128,128]{2,1,0:T(8,128)S(1)} %get-tuple-element.74), custom_call_target="InvertDiagBlocksLowerTriangular" | custom-call | tf_op jit(solution)/shard_map/jit(cholesky)/cholesky | solution.py:17
  372.7 11.7 %cholesky.506 = f32[128,128]{1,0:T(8,128)S(1)} custom-call(f32[128,128]{1,0:T(8,128)S(1)} %cholesky.599), custom_call_target="Cholesky" | custom-call | tf_op jit(solution)/shard_map/jit(cholesky)/cholesky | solution.py:17
  385.7 10.0 %custom-call.67 = f32[1,128,128]{1,2,0:T(8,128)S(1)} custom-call(f32[1,128,128]{2,1,0:T(8,128)S(1)} %get-tuple-element.71), custom_call_target="InvertDiagBlocksLowerTriangular" | custom-call | tf_op jit(solution)/shard_map/jit(cholesky)/cholesky | solution.py:17
  399.0 11.7 %cholesky.526 = f32[128,128]{1,0:T(8,128)S(1)} custom-call(f32[128,128]{1,0:T(8,128)S(1)} %cholesky.604), custom_call_target="Cholesky" | custom-call | tf_op jit(solution)/shard_map/jit(cholesky)/cholesky | solution.py:17
  412.0 9.8 %custom-call.68 = f32[1,128,128]{1,2,0:T(8,128)S(1)} custom-call(f32[1,128,128]{2,1,0:T(8,128)S(1)} %get-tuple-element.68), custom_call_target="InvertDiagBlocksLowerTriangular" | custom-call | tf_op jit(solution)/shard_map/jit(cholesky)/cholesky | solution.py:17
  424.8 12.1 %cholesky.546 = f32[128,128]{1,0:T(8,128)S(1)} custom-call(f32[128,128]{1,0:T(8,128)S(1)} %cholesky.609), custom_call_target="Cholesky" | custom-call | tf_op jit(solution)/shard_map/jit(cholesky)/cholesky | solution.py:17
  438.2 9.8 %custom-call.69 = f32[1,128,128]{1,2,0:T(8,128)S(1)} custom-call(f32[1,128,128]{2,1,0:T(8,128)S(1)} %get-tuple-element.65), custom_call_target="InvertDiagBlocksLowerTriangular" | custom-call | tf_op jit(solution)/shard_map/jit(cholesky)/cholesky | solution.py:17
  450.7 11.7 %cholesky.564 = f32[128,128]{1,0:T(8,128)S(1)} custom-call(f32[128,128]{1,0:T(8,128)S(1)} %convolution_subtract_fusion.11), custom_call_target="Cholesky" | custom-call | tf_op jit(solution)/shard_map/jit(cholesky)/cholesky | solution.py:17
  468.6 6.7 multiply_bitcast_fusion
  480.6 23.4 %while.1 = (s32[]{:T(128)}, f32[1024,1024]{1,0:T(8,128)}, s32[8,2]{0,1:T(2,128)S(1)}, f32[8,128,128]{2,1,0:T(8,128)S(1)}, s32[]{:T(128)}) while((s32[]{:T(128)}, f32[1024,1024]{1,0:T(8,128)}, s32[8,2]{0,1:T(2,128)S(1)}, f32[8,128,128]{2,1,0:T(8,128)S(1)}, s32[]{:T(128)}) %tuple.74), condition=%wide.while_cond, body=%wide.while_body.sunk | while | flops 2 | bytes 131189 | solution.py:21
  504.1 78.8 %custom-call.70 = f32[8,128,128]{1,2,0:T(8,128)S(1)} custom-call(f32[8,128,128]{2,1,0:T(8,128)S(1)} %get-tuple-element.9), custom_call_target="InvertDiagBlocksLowerTriangular" | custom-call | tf_op jit(solution)/shard_map/jit(_solve_triangular)/triangular_solve | solution.py:21
  618.1 6.4 fusion.21
  630.8 9.3 %convolution_subtract_fusion.1 = f32[128,4096]{1,0:T(8,128)S(1)} fusion(f32[640,4096]{1,0:T(8,128)} %get-tuple-element.45, f32[1024,4096]{1,0:T(8,128)S(1)} %bitcast.131, f32[1024,1024]{1,0:T(8,128)} %get-tuple-element.145), kind=kOutput, calls=%fused_computation.27 | convolution fusion | flops 4027056128 | bytes 15007744 | tf_op jit(solution)/shard_map/jit(_solve_triangular)/triangular_solve | solution.py:21
  645.7 9.8 %convolution_subtract_fusion = f32[128,4096]{1,0:T(8,128)S(1)} fusion(f32[768,4096]{1,0:T(8,128)} %get-tuple-element.41, f32[1024,4096]{1,0:T(8,128)S(1)} %bitcast.131, f32[1024,1024]{1,0:T(8,128)} %get-tuple-element.145), kind=kOutput, calls=%fused_computation.26 | convolution fusion | flops 4832362496 | bytes 17170432 | tf_op jit(solution)/shard_map/jit(_solve_triangular)/triangular_solve | solution.py:21
  660.3 11.7 %convolution_subtract_fusion.4 = f32[128,4096]{1,0:T(8,128)S(1)} fusion(f32[896,4096]{1,0:T(8,128)} %get-tuple-element.37, f32[1024,4096]{1,0:T(8,128)S(1)} %bitcast.131, f32[1024,1024]{1,0:T(8,128)} %get-tuple-element.145), kind=kOutput, calls=%fused_computation.30 | convolution fusion | flops 5637668864 | bytes 19333120 | tf_op jit(solution)/shard_map/jit(_solve_triangular)/triangular_solve | solution.py:21
  676.2 9.2 %fusion = bf16[4096,1024]{0,1:T(8,128)(2,1)} fusion(f32[1024,4096]{1,0:T(8,128)} %convolution_dynamic-update-slice_fusion), kind=kLoop, calls=%fused_computation.6 | loop fusion | flops 8388608 | bytes 25165824 | tf_op jit(solution)/shard_map/convert_element_type | solution.py:24
  685.4 11.9 %copy.27 = bf16[4096,1024]{1,0:T(8,128)(2,1)} copy(bf16[4096,1024]{0,1:T(8,128)(2,1)} %fusion) | data formatting | bytes 16777216
  (113 shorter events, 141.2 us)
Async XLA Ops:
  16.0 55.5 %all-to-all-start = ((bf16[8,128,1024]{2,1,0:T(8,128)(2,1)}), bf16[8,128,1024]{2,1,0:T(8,128)(2,1)S(1)}, u32[]{:S(2)}, u32[]{:S(2)}) async-start(bf16[8,128,1024]{2,1,0:T(8,128)(2,1)} %broadcast_select_fusion), calls=%async_computation | async-start | bytes 4194304 | tf_op jit(solution)/shard_map/all_to_all | solution.py:61
  23.3 229.4 %all-reduce.3.cloned.1.call-start = ((), (), s32[]{:S(2)}) async-start(), calls=%async_computation.1 | async-start | bytes 8388608 | tf_op jit(solution)/shard_map/psum | solution.py:16
  262.7 1.9 copy-start
  582.8 29.7 %copy-start.1 = (f32[8,128,128]{1,2,0:T(8,128)}, f32[8,128,128]{1,2,0:T(8,128)S(1)}, u32[]{:S(2)}) copy-start(f32[8,128,128]{1,2,0:T(8,128)S(1)} %custom-call.70) | copy-start | bytes 1572868
  582.8 15.6 %slice-start = ((s8[16777216]{0:T(1024)(128)(4,1)}), s8[4194304]{0:T(1024)(128)(4,1)S(1)}, s32[]{:S(2)}) async-start(s8[16777216]{0:T(1024)(128)(4,1)} %bitcast.130), calls=%async_computation.2 | async-start | bytes 8388608
  582.9 15.6 %slice-start.1 = ((s8[16777216]{0:T(1024)(128)(4,1)}), s8[4194304]{0:T(1024)(128)(4,1)S(1)}, s32[]{:S(2)}) async-start(s8[16777216]{0:T(1024)(128)(4,1)} %bitcast.130), calls=%async_computation.3 | async-start | bytes 8388608
  589.0 9.5 %slice-start.2 = ((s8[16777216]{0:T(1024)(128)(4,1)}), s8[4194304]{0:T(1024)(128)(4,1)S(1)}, s32[]{:S(2)}) async-start(s8[16777216]{0:T(1024)(128)(4,1)} %bitcast.130), calls=%async_computation.4 | async-start | bytes 8388608
  592.7 5.8 slice-start.3
Sparse Core Ops, SparseCore 0:
  111.1 141.5 all-reduce.2
where the time goes:
time: 712 us; the launch traced here: 704 us
  other arithmetic  301 us (42%)
  waiting for transfers between devices  166 us (23%)
  matrix products  132 us (19%)
  local copies, waits for them, and re-layouts  77.8 us (11%)
  between operations  19.5 us (3%)
  starting transfers between devices  7.32 us (1%)
    another operation x31, other arithmetic, factor(): return jnp.linalg.cholesky(summed)  173 us
    psum x1, waiting for transfers between devices, factor(): summed = lax.psum(gram_local, ('gx', 'gy'))  119 us
    another operation x15, matrix products, normalise(): jax.scipy.linalg.solve_triangular(low_factor, row_block.astype(jnp.float3...  93.2 us
    another operation x2, other arithmetic, normalise(): jax.scipy.linalg.solve_triangular(low_factor, row_block.astype(jnp.float3...  78.8 us
    all_to_all x1, waiting for transfers between devices, on_device(): lax.all_to_all(jnp.where(send_has[:, None, None], tile_stack[send_index],...  47.7 us
    another operation x24, local copies, waits for them, and re-layouts  23.3 us
    another operation x14, matrix products, factor(): return jnp.linalg.cholesky(summed)  23 us
    gather x2, local copies, waits for them, and re-layouts, on_device(): combined[source]  21.7 us
  transfers between devices with their start and end apart: 2, of which 2 were waited for; matrix products, arithmetic and copies ran while one was open for 3% of the time, Pallas kernels for 0%

commit v1 on v0

v1 whole, which is shorter than its diff:
```python
import functools
import math

import jax
import jax.numpy as jnp
from jax import lax
from jax.experimental import pallas as pl
from jax.experimental.pallas import tpu as pltpu
from jax.sharding import PartitionSpec as P

TILE = 128
SLOTS = 32
GROUP = 4
BIG = 256
PANEL = 4
NT = (((1,), (1,)), ((), ()))
TN = (((0,), (0,)), ((), ()))
HIGHEST = lax.Precision.HIGHEST


def gram_kernel(height_ref, a_ref, out_ref):
    step = pl.program_id(0)
    rows, breadth = a_ref.shape
    live = height_ref[0] * TILE - step * rows

    @pl.when(step == 0)
    def _():
        out_ref[...] = jnp.zeros_like(out_ref)

    def add(block):
        across = block.T
        place = 0
        for i in range(breadth // BIG):
            width = (i + 1) * BIG
            product = lax.dot_general(
                across[i * BIG : (i + 1) * BIG],
                block[:, :width],
                (((1,), (0,)), ((), ())),
                preferred_element_type=jnp.float32,
            )
            for j in range(i + 1):
                out_ref[place] += product[:, j * BIG : (j + 1) * BIG]
                place += 1

    @pl.when(live >= rows)
    def _():
        add(a_ref[...])

    @pl.when((live > 0) & (live < rows))
    def _():
        index = lax.broadcasted_iota(jnp.int32, (rows, breadth), 0)
        keep = (index < live).astype(jnp.float32).astype(a_ref.dtype)
        add(a_ref[...] * keep)


def local_gram(a_rows, height):
    total, breadth = a_rows.shape
    rows = GROUP * TILE
    blocks = breadth // BIG
    packed = blocks * (blocks + 1) // 2
    return pl.pallas_call(
        gram_kernel,
        out_shape=jax.ShapeDtypeStruct((packed, BIG, BIG), jnp.float32),
        grid_spec=pltpu.PrefetchScalarGridSpec(
            num_scalar_prefetch=1,
            grid=(total // rows,),
            in_specs=[
                pl.BlockSpec(
                    (rows, breadth),
                    lambda i, h: (jnp.minimum(i, (h[0] - 1) // GROUP), 0),
                )
            ],
            out_specs=pl.BlockSpec((packed, BIG, BIG), lambda i, h: (0, 0, 0)),
        ),
        cost_estimate=pl.CostEstimate(
            flops=total * breadth * breadth, bytes_accessed=total * breadth * 2, transcendentals=0
        ),
        name="gram",
    )(height, a_rows)


def eliminate(block):
    lane = lax.broadcasted_iota(jnp.int32, (1, TILE), 1)
    sub = lax.broadcasted_iota(jnp.int32, (8, TILE), 0)
    parts = [block[8 * g : 8 * g + 8] for g in range(TILE // 8)]
    for first in range(0, TILE, PANEL):
        start = first // 8
        spread = [
            [jnp.broadcast_to(part[:, first + m : first + m + 1], (8, TILE)) for part in parts[start:]]
            for m in range(PANEL)
        ]
        for m in range(PANEL):
            at = first + m
            local = at % 8
            column = spread[m]
            pivot = jnp.broadcast_to(column[0][local : local + 1], (8, TILE))
            inverse = 1.0 / pivot
            factors = [c * inverse for c in column]
            below = sub > local
            factors[0] = jnp.where(below, factors[0], 0.0)
            here = lane == at
            row = jnp.where(here, 1.0, parts[start][local : local + 1])
            row = jnp.broadcast_to(row, (8, TILE))
            for g in range(start, len(parts)):
                clear = here & below if g == start else here
                parts[g] = jnp.where(clear, 0.0, parts[g]) - factors[g - start] * row
            for n in range(m + 1, PANEL):
                level = jnp.broadcast_to(spread[n][0][local : local + 1], (8, TILE))
                spread[n] = [c - f * level for c, f in zip(spread[n], factors)]
    return jnp.concatenate(parts, axis=0)


def factor_kernel(root_scale, gram_ref, r_ref, high_ref, low_ref, work, line):
    breadth = r_ref.shape[0]
    count = breadth // TILE
    place = 0
    for i in range(breadth // BIG):
        for j in range(i + 1):
            block = gram_ref[place]
            work[i * BIG : (i + 1) * BIG, j * BIG : (j + 1) * BIG] = block
            if j < i:
                work[j * BIG : (j + 1) * BIG, i * BIG : (i + 1) * BIG] = block.T
            place += 1
    rows_id = lax.broadcasted_iota(jnp.int32, (TILE, TILE), 0)
    cols_id = lax.broadcasted_iota(jnp.int32, (TILE, TILE), 1)
    wide_id = lax.broadcasted_iota(jnp.int32, (TILE, breadth), 1)

    def step(k, carry):
        base = pl.multiple_of(k * TILE, TILE)
        mine = pl.ds(base, TILE)
        done = eliminate(work[mine, mine])
        diagonal = jnp.sum(jnp.where(rows_id == cols_id, done, 0.0), axis=1, keepdims=True)
        shrink = 1.0 / jnp.sqrt(diagonal)
        inverse = jnp.where(
            rows_id > cols_id, done, jnp.where(rows_id == cols_id, 1.0, 0.0)
        ) * shrink
        upper = jnp.where(rows_id <= cols_id, done, 0.0) * shrink
        line[...] = jnp.dot(
            inverse, work[mine, :], precision=HIGHEST, preferred_element_type=jnp.float32
        )
        r_ref[mine, :] = jnp.where(wide_id >= base, line[...], 0.0) * (1.0 / root_scale)
        r_ref[mine, mine] = upper * (1.0 / root_scale)
        line[:, mine] = inverse
        solved = jnp.where(wide_id < base + TILE, line[...], 0.0)
        high = solved.astype(jnp.bfloat16)
        high_ref[mine, :] = high
        low_ref[mine, :] = (solved - high.astype(jnp.float32)).astype(jnp.bfloat16)

        def update(i, carry):
            theirs = pl.ds(pl.multiple_of(i * TILE, TILE), TILE)
            left = lax.dot_general(
                work[theirs, mine], inverse, NT, precision=HIGHEST, preferred_element_type=jnp.float32
            )
            work[theirs, mine] = jnp.zeros((TILE, TILE), jnp.float32)
            work[theirs, :] -= jnp.dot(
                left, line[...], precision=HIGHEST, preferred_element_type=jnp.float32
            )
            return carry

        lax.fori_loop(k + 1, count, update, 0)
        return carry

    lax.fori_loop(0, count, step, 0)


def factor(packed, breadth, root_scale):
    square = (breadth, breadth)
    return pl.pallas_call(
        functools.partial(factor_kernel, root_scale),
        out_shape=(
            jax.ShapeDtypeStruct(square, jnp.float32),
            jax.ShapeDtypeStruct(square, jnp.bfloat16),
            jax.ShapeDtypeStruct(square, jnp.bfloat16),
        ),
        in_specs=[pl.BlockSpec(memory_space=pltpu.VMEM)],
        out_specs=tuple(pl.BlockSpec(memory_space=pltpu.VMEM) for _ in range(3)),
        scratch_shapes=[
            pltpu.VMEM(square, jnp.float32),
            pltpu.VMEM((TILE, breadth), jnp.float32),
        ],
        name="factor",
    )(packed)


def ortho_kernel(root_scale, own_at, in_at, kind, *refs):
    own, come = refs[:GROUP], refs[GROUP : 2 * GROUP]
    high_ref, low_ref, out_ref, block = refs[2 * GROUP :]
    step = pl.program_id(0)
    breadth = out_ref.shape[1]
    for g in range(GROUP):
        which = kind[step * GROUP + g]
        rows = pl.ds(g * TILE, TILE)

        @pl.when(which == 0)
        def _():
            block[rows, :] = jnp.zeros((TILE, breadth), block.dtype)

        @pl.when(which == 1)
        def _():
            block[rows, :] = own[g][...]

        @pl.when(which == 2)
        def _():
            block[rows, :] = come[g][...]

    for j in range(breadth // BIG):
        cols = slice(j * BIG, (j + 1) * BIG)
        width = (j + 1) * BIG
        left = block[:, :width]
        product = lax.dot_general(
            left, high_ref[cols, :width], NT, preferred_element_type=jnp.float32
        ) + lax.dot_general(left, low_ref[cols, :width], NT, preferred_element_type=jnp.float32)
        out_ref[:, cols] = (product * root_scale).astype(out_ref.dtype)


def carried(index, used):
    index = index.reshape(-1, GROUP)
    used = used.reshape(-1, GROUP)
    steps = jnp.arange(index.shape[0], dtype=jnp.int32)
    earlier = used[None, :, :] & (steps[None, :, None] <= steps[:, None, None])
    last = jnp.max(jnp.where(earlier, steps[None, :, None], -1), axis=1)
    pick = last[:, None, :] == steps[None, :, None]
    return jnp.sum(jnp.where(pick, index[None], 0), axis=1).reshape(-1)


def orthonormal(a_rows, received, own_at, in_at, kind, high, low, root_scale):
    breadth = a_rows.shape[1]
    rows = GROUP * TILE

    def own_spec(g):
        return pl.BlockSpec((TILE, breadth), lambda s, o, c, k: (o[s * GROUP + g], 0))

    def in_spec(g):
        return pl.BlockSpec((TILE, breadth), lambda s, o, c, k: (c[s * GROUP + g], 0))

    whole = pl.BlockSpec((breadth, breadth), lambda s, o, c, k: (0, 0))
    return pl.pallas_call(
        functools.partial(ortho_kernel, root_scale),
        out_shape=jax.ShapeDtypeStruct((SLOTS * TILE, breadth), a_rows.dtype),
        grid_spec=pltpu.PrefetchScalarGridSpec(
            num_scalar_prefetch=3,
            grid=(SLOTS // GROUP,),
            in_specs=[own_spec(g) for g in range(GROUP)]
            + [in_spec(g) for g in range(GROUP)]
            + [whole, whole],
            out_specs=pl.BlockSpec((rows, breadth), lambda s, o, c, k: (s, 0)),
            scratch_shapes=[pltpu.VMEM((rows, breadth), a_rows.dtype)],
        ),
        name="ortho",
    )(own_at, in_at, kind, *([a_rows] * GROUP), *([received] * GROUP), high, low)


def on_device(a_rows, heights, destination):
    breadth = a_rows.shape[1]
    size_gy = lax.axis_size("gy")
    devices = lax.axis_size("gx") * size_gy
    group_pos = lax.axis_index("gy")
    my_index = lax.axis_index("gx") * size_gy + group_pos
    group_base = my_index - group_pos
    tile_stack = a_rows.reshape(-1, TILE, breadth)
    stored = tile_stack.shape[0]
    tile_ids = jnp.arange(stored, dtype=jnp.int32)
    peer_ids = jnp.arange(size_gy, dtype=jnp.int32)
    slot_ids = jnp.arange(SLOTS, dtype=jnp.int32)
    tile_live = tile_ids[None, :] < heights[:, None]
    target_dev = destination // SLOTS
    target_slot = destination % SLOTS
    own_live = tile_live[group_pos]
    own_dev = target_dev[group_pos]
    own_slot = target_slot[group_pos]
    leaving = own_live & (own_dev != my_index)
    chosen = leaving[None, :] & (own_dev[None, :] - group_base == peer_ids[:, None])
    send_index = jnp.sum(jnp.where(chosen, tile_ids[None, :], 0), axis=1)
    arriving = tile_live & (target_dev == my_index) & (peer_ids[:, None] != group_pos)
    arrive_slot = jnp.sum(jnp.where(arriving, target_slot, 0), axis=1)
    arrive_has = jnp.any(arriving, axis=1)
    staying = own_live & (own_dev == my_index)
    own_match = staying[None, :] & (own_slot[None, :] == slot_ids[:, None])
    in_match = arrive_has[None, :] & (arrive_slot[None, :] == slot_ids[:, None])
    own_has = jnp.any(own_match, axis=1)
    in_has = jnp.any(in_match, axis=1)
    own_at = carried(jnp.sum(jnp.where(own_match, tile_ids[None, :], 0), axis=1), own_has)
    in_at = carried(jnp.sum(jnp.where(in_match, peer_ids[None, :], 0), axis=1), in_has)
    kind = jnp.where(own_has, 1, jnp.where(in_has, 2, 0)).astype(jnp.int32)
    root_scale = math.sqrt(devices * SLOTS * TILE)
    received = lax.all_to_all(
        tile_stack[send_index], "gy", split_axis=0, concat_axis=0, tiled=True
    ).reshape(-1, breadth)
    packed = local_gram(a_rows, lax.dynamic_slice(heights, (group_pos,), (1,)))
    packed = lax.psum(packed, ("gx", "gy"))
    factor_r, high, low = factor(packed, breadth, root_scale)
    ortho_rows = orthonormal(a_rows, received, own_at, in_at, kind, high, low, root_scale)
    return (ortho_rows, factor_r)


def solution(mesh):
    placed = (P(("gx", "gy"), None), P("gx"), P("gx", None))
    return jax.shard_map(
        on_device,
        mesh=mesh,
        in_specs=placed,
        out_specs=(P(("gx", "gy"), None), P()),
        check_vma=False,
    )
```

time: 712 us -> 297 us (0.42)
  other arithmetic: 301 us -> 2.7 us
  matrix products: 132 us -> 0 us
  Pallas kernels: 0 us -> 110 us
  local copies, waits for them, and re-layouts: 77.8 us -> 11.4 us
  waiting for transfers between devices: 166 us -> 150 us
    another operation x33 -> x0, other arithmetic: 252 us -> none  [the longest x31 173 us: factor(): return jnp.linalg.cholesky(summed)]
    another operation x29 -> x0, matrix products: 116 us -> none  [the longest x15 93.2 us: normalise(): jax.scipy.linalg.solve_triangular(low_factor, row_block.astype(jnp.float3...]
    pallas_call x0 -> x3, Pallas kernels: none -> 110 us  [the longest x1 80 us: factor(): pl.pallas_call(functools.partial(factor_kernel, root_scale), out_shape=(j...]
    all_to_all x1, waiting for transfers between devices: 47.7 us -> 0.01 us  [on_device(): lax.all_to_all(tile_stack[send_index], 'gy', split_axis=0, concat_axis=0,...]
    psum x1, waiting for transfers between devices: 119 us -> 150 us  [on_device(): packed = lax.psum(packed, ('gx', 'gy'))]
    another operation x33 -> x0, local copies, waits for them, and re-layouts: 25.9 us -> none
    gather x2 -> x0, local copies, waits for them, and re-layouts: 21.7 us -> none  [on_device(): combined[source]]
    unnamed x14 -> x6, local copies, waits for them, and re-layouts: 19.2 us -> 2.02 us
  transfers between devices with their start and end apart: 2 -> 2, of which waited for: 2 -> 1; matrix products, arithmetic and copies ran while one was open for 3% -> 2% of each run, Pallas kernels for 0% -> 31%
where the time goes in v1:
time: 297 us; the launch traced here: 296 us
  waiting for transfers between devices  150 us (51%)
  Pallas kernels  110 us (37%)
  between operations  14.1 us (5%)
  local copies, waits for them, and re-layouts  11.4 us (4%)
  starting transfers between devices  7.45 us (3%)
    psum x1, waiting for transfers between devices, on_device(): packed = lax.psum(packed, ('gx', 'gy'))  150 us
    pallas_call x1, Pallas kernels, factor(): pl.pallas_call(functools.partial(factor_kernel, root_scale), out_shape=(j...  80 us
    pallas_call x1, Pallas kernels, orthonormal(): pl.pallas_call(functools.partial(ortho_kernel, root_scale), out_shape=jax...  19.3 us
    pallas_call x1, Pallas kernels, local_gram(): pl.pallas_call(gram_kernel, out_shape=jax.ShapeDtypeStruct((packed, BIG,...  11.2 us
    all_to_all x1, starting transfers between devices, on_device(): lax.all_to_all(tile_stack[send_index], 'gy', split_axis=0, concat_axis=0,...  7.41 us
    gather x1, local copies, waits for them, and re-layouts, on_device(): tile_stack[send_index]  6.58 us
  transfers between devices with their start and end apart: 2, of which 1 were waited for; matrix products, arithmetic and copies ran while one was open for 2% of the time, Pallas kernels for 31%

profile of v1, /device:TPU:0, one launch (start us, length us, event | category | flops | bytes accessed | tf_op | source)
XLA Modules:
  0.0 296.4 jit_solution(7790510132488887029)
XLA Ops:
  7.2 0.9 fusion.9
  8.1 0.1 select_reduce_fusion.5
  8.2 6.6 %gather_fusion = bf16[8,128,1024]{2,1,0:T(8,128)(2,1)} fusion(bf16[48,128,1024]{2,1,0:T(8,128)(2,1)} %bitcast.14, s32[1024]{0:T(1024)S(1)} %pad_clamp_fusion), kind=kCustom, calls=%fused_computation | custom fusion | bytes 4194336 | tf_op jit(solution)/shard_map/gather | solution.py:287
  14.8 7.4 %all-to-all-start = ((bf16[8,128,1024]{2,1,0:T(8,128)(2,1)}), bf16[8,128,1024]{2,1,0:T(8,128)(2,1)S(1)}, u32[]{:S(2)}, u32[]{:S(2)}) async-start(bf16[8,128,1024]{2,1,0:T(8,128)(2,1)} %gather_fusion), calls=%async_computation | async-start | bytes 4194304 | tf_op jit(solution)/shard_map/all_to_all | solution.py:286
  22.2 0.0 all-reduce.2.cloned.1.call-start
  22.3 0.7 dynamic_slice.15.height_ref
  23.0 11.2 %gram.1 = f32[10,256,256]{2,1,0:T(8,128)} custom-call(s32[1]{0:T(128)} %dynamic_slice.15.height_ref, bf16[6144,1024]{1,0:T(8,128)(2,1)} %refs_3_.1), custom_call_target="tpu_custom_call" | custom-call | flops 6442450944 | bytes 12582912 | tf_op jit(solution)/shard_map/gram/pallas_call | solution.py:61
  34.2 0.7 copy-done.1
  34.8 0.1 select_reduce_fusion.7
  35.0 0.1 fusion.4
  35.0 0.1 and.104
  35.1 0.1 copy.8
  35.2 0.1 fusion.1
  35.4 0.1 and.95
  35.4 0.1 copy.5
  35.5 0.1 select_reduce_fusion.6
  35.6 0.1 broadcast_in_dim.126
  35.7 0.1 copy.9
  35.8 0.1 select_reduce_fusion.3
  35.9 0.1 broadcast_in_dim.119
  36.0 0.1 copy.6
  36.1 0.2 select_reduce_fusion.1
  36.3 0.3 select_reduce_fusion
  36.6 0.1 copy.10
  36.7 0.6 reshape.59.in_at
  37.3 0.1 copy.7
  37.4 0.7 reshape.58.own_at
  38.1 0.6 select_select_fusion.kind
  38.6 150.3 %all-reduce.2.cloned.1.call-done.gram_ref = f32[10,256,256]{2,1,0:T(8,128)} async-done(((f32[10,256,256]{2,1,0:T(8,128)}), f32[10,256,256]{2,1,0:T(8,128)}) %all-reduce.2.cloned.1.call-update) | async-done | bytes 2621456 | tf_op jit(solution)/shard_map/psum | solution.py:290
  188.9 80.0 %factor.1 = (f32[1024,1024]{1,0:T(8,128)}, bf16[1024,1024]{1,0:T(8,128)(2,1)}, bf16[1024,1024]{1,0:T(8,128)(2,1)}) custom-call(f32[10,256,256]{2,1,0:T(8,128)} %all-reduce.2.cloned.1.call-done.gram_ref), custom_call_target="tpu_custom_call" | custom-call | tf_op jit(solution)/shard_map/factor/pallas_call | solution.py:168
  268.9 1.4 copy-done
  270.3 19.3 %ortho.1 = bf16[4096,1024]{1,0:T(8,128)(2,1)} custom-call(s32[32]{0:T(128)} %reshape.58.own_at, s32[32]{0:T(128)} %reshape.59.in_at, s32[32]{0:T(128)} %select_select_fusion.kind, bf16[6144,1024]{1,0:T(8,128)(2,1)} %refs_3_.1, bf16[6144,1024]{1,0:T(8,128)(2,1)} %refs_3_.1, bf16[6144,1024]{1,0:T(8,128)(2,1)} %refs_3_.1, bf16[6144,1024]{1,0:T(8,128)(2,1)} %refs_3_.1, ...), custom_call_target="tpu_custom_call" | custom-call | tf_op jit(solution)/shard_map/ortho/pallas_call | solution.py:237
  (13 shorter events, 0.1 us)
Async XLA Ops:
  14.8 7.5 %copy-start.2 = (s32[8]{0:T(128)S(1)}, s32[8]{0:T(128)}, u32[]{:S(2)}) copy-start(s32[8]{0:T(128)} %param.4) | copy-start | bytes 100
  14.8 254.1 %all-to-all-start = ((bf16[8,128,1024]{2,1,0:T(8,128)(2,1)}), bf16[8,128,1024]{2,1,0:T(8,128)(2,1)S(1)}, u32[]{:S(2)}, u32[]{:S(2)}) async-start(bf16[8,128,1024]{2,1,0:T(8,128)(2,1)} %gather_fusion), calls=%async_computation | async-start | bytes 4194304 | tf_op jit(solution)/shard_map/all_to_all | solution.py:286
  22.2 166.7 %all-reduce.2.cloned.1.call-start = ((), (), s32[]{:S(2)}) async-start(), calls=%async_computation.1 | async-start | bytes 5242880 | tf_op jit(solution)/shard_map/psum | solution.py:290
  34.1 0.7 copy-start.1
  268.9 1.4 copy-start
Sparse Core Ops, SparseCore 0:
  34.3 154.6 all-reduce.1

commit v2 on v1

--- a/solution.py
+++ b/solution.py
@@ -12,7 +12,8 @@
 SLOTS = 32
 GROUP = 4
 BIG = 256
-PANEL = 4
+PANEL = 8
+REGS = TILE // 8
 NT = (((1,), (1,)), ((), ()))
 TN = (((0,), (0,)), ((), ()))
 HIGHEST = lax.Precision.HIGHEST
@@ -38,9 +39,11 @@
                 (((1,), (0,)), ((), ())),
                 preferred_element_type=jnp.float32,
             )
-            for j in range(i + 1):
-                out_ref[place] += product[:, j * BIG : (j + 1) * BIG]
-                place += 1
+            for top in range(0, BIG, TILE):
+                for j in range((i * BIG + top) // TILE + 1):
+                    piece = product[top : top + TILE, j * TILE : (j + 1) * TILE]
+                    out_ref[place : place + REGS] += piece.reshape(REGS, 8, TILE)
+                    place += REGS
 
     @pl.when(live >= rows)
     def _():
@@ -53,14 +56,14 @@
         add(a_ref[...] * keep)
 
 
-def local_gram(a_rows, height):
+def local_gram(a_rows, height, split):
     total, breadth = a_rows.shape
     rows = GROUP * TILE
-    blocks = breadth // BIG
-    packed = blocks * (blocks + 1) // 2
+    blocks = breadth // TILE
+    packed = pl.cdiv(blocks * (blocks + 1) // 2 * REGS, split) * split
     return pl.pallas_call(
         gram_kernel,
-        out_shape=jax.ShapeDtypeStruct((packed, BIG, BIG), jnp.float32),
+        out_shape=jax.ShapeDtypeStruct((packed, 8, TILE), jnp.float32),
         grid_spec=pltpu.PrefetchScalarGridSpec(
             num_scalar_prefetch=1,
             grid=(total // rows,),
@@ -70,7 +73,7 @@
                     lambda i, h: (jnp.minimum(i, (h[0] - 1) // GROUP), 0),
                 )
             ],
-            out_specs=pl.BlockSpec((packed, BIG, BIG), lambda i, h: (0, 0, 0)),
+            out_specs=pl.BlockSpec((packed, 8, TILE), lambda i, h: (0, 0, 0)),
         ),
         cost_estimate=pl.CostEstimate(
             flops=total * breadth * breadth, bytes_accessed=total * breadth * 2, transcendentals=0
@@ -114,13 +117,13 @@
     breadth = r_ref.shape[0]
     count = breadth // TILE
     place = 0
-    for i in range(breadth // BIG):
+    for i in range(count):
         for j in range(i + 1):
-            block = gram_ref[place]
-            work[i * BIG : (i + 1) * BIG, j * BIG : (j + 1) * BIG] = block
+            block = gram_ref[place : place + REGS].reshape(TILE, TILE)
+            work[i * TILE : (i + 1) * TILE, j * TILE : (j + 1) * TILE] = block
             if j < i:
-                work[j * BIG : (j + 1) * BIG, i * BIG : (i + 1) * BIG] = block.T
-            place += 1
+                work[j * TILE : (j + 1) * TILE, i * TILE : (i + 1) * TILE] = block.T
+            place += REGS
     rows_id = lax.broadcasted_iota(jnp.int32, (TILE, TILE), 0)
     cols_id = lax.broadcasted_iota(jnp.int32, (TILE, TILE), 1)
     wide_id = lax.broadcasted_iota(jnp.int32, (TILE, breadth), 1)
@@ -163,6 +166,146 @@
     lax.fori_loop(0, count, step, 0)
 
 
+def reduce_kernel(sizes, x_ref, out_ref, work, *rest):
+    streams = (("core", "x", "y", "z"), ("core", "y", "x", "z"))
+    depth = len(streams[0])
+    arrived, sends, recvs = rest[: 2 * depth], rest[2 * depth], rest[2 * depth + 1]
+    at_gx, at_gy = lax.axis_index("gx"), lax.axis_index("gy")
+    pair, across = sizes["core"], sizes["x"]
+    here = {
+        "core": lax.rem(at_gx, pair),
+        "y": lax.div(at_gx, pair),
+        "x": lax.rem(at_gy, across),
+        "z": lax.div(at_gy, across),
+    }
+
+    def peer(dim, offset):
+        there = dict(here)
+        there[dim] = lax.rem(here[dim] + offset, sizes[dim])
+        where = (there["y"] * pair + there["core"], there["z"] * across + there["x"])
+        return there[dim], where
+
+    barrier = pltpu.get_barrier_semaphore()
+    greeted = 0
+    for dim in streams[0]:
+        for offset in range(1, sizes[dim]):
+            pl.semaphore_signal(
+                barrier, inc=1, device_id=peer(dim, offset)[1], device_id_type=pl.DeviceIdType.MESH
+            )
+            greeted += 1
+    pl.semaphore_wait(barrier, greeted)
+
+    half = x_ref.shape[0] // 2
+    used = [0]
+
+    def send(source, target, where):
+        slot = used[0]
+        used[0] += 1
+        copy = pltpu.make_async_remote_copy(
+            src_ref=source,
+            dst_ref=target,
+            send_sem=sends.at[slot],
+            recv_sem=recvs.at[slot],
+            device_id=where,
+            device_id_type=pl.DeviceIdType.MESH,
+        )
+        copy.start()
+        return copy
+
+    pending = []
+    base = [0, half]
+    size = [half, half]
+    bases = [[], []]
+
+    def scatter(s, level):
+        dim = streams[s][level]
+        part = size[s] // sizes[dim]
+        source = x_ref if level == 0 else work
+        copies = []
+        for offset in range(1, sizes[dim]):
+            index, where = peer(dim, offset)
+            copies.append(
+                send(
+                    source.at[pl.ds(base[s] + index * part, part)],
+                    arrived[s * depth + level].at[offset - 1],
+                    where,
+                )
+            )
+        return copies
+
+    def collect(s, level, copies):
+        dim = streams[s][level]
+        part = size[s] // sizes[dim]
+        source = x_ref if level == 0 else work
+        target = out_ref if level == depth - 1 else work
+        mine = pl.ds(base[s] + here[dim] * part, part)
+        for copy in copies:
+            copy.wait_recv()
+        total = source[mine]
+        for offset in range(1, sizes[dim]):
+            total += arrived[s * depth + level][offset - 1]
+        target[mine] = total
+        pending.extend(copies)
+        base[s] = base[s] + here[dim] * part
+        size[s] = part
+        bases[s].append((base[s], part))
+
+    def gather(s, level):
+        start, part = bases[s][level]
+        dim = streams[s][level]
+        mine = out_ref.at[pl.ds(start, part)]
+        return [send(mine, mine, peer(dim, offset)[1]) for offset in range(1, sizes[dim])]
+
+    def landed(copies):
+        for copy in copies:
+            copy.wait_recv()
+        pending.extend(copies)
+
+    flying = [scatter(s, 0) for s in range(2)]
+    for level in range(depth):
+        for s in range(2):
+            collect(s, level, flying[s])
+            flying[s] = scatter(s, level + 1) if level + 1 < depth else gather(s, level)
+    for level in reversed(range(depth)):
+        for s in range(2):
+            landed(flying[s])
+            if level:
+                flying[s] = gather(s, level - 1)
+    for copy in pending:
+        copy.wait_send()
+
+
+def grid_sizes():
+    size_gx, size_gy = lax.axis_size("gx"), lax.axis_size("gy")
+    across = 1
+    while across * across * 4 <= size_gy and size_gy % (across * 2) == 0:
+        across *= 2
+    pair = 2 if size_gx % 2 == 0 else 1
+    return {"core": pair, "y": size_gx // pair, "x": across, "z": size_gy // across}
+
+
+def reduce_all(packed, sizes):
+    part = packed.shape[0] // 2
+    buffers = []
+    for order in (("core", "x", "y", "z"), ("core", "y", "x", "z")):
+        left = part
+        for dim in order:
+            left //= sizes[dim]
+            buffers.append(pltpu.VMEM((max(sizes[dim] - 1, 1), left, 8, TILE), jnp.float32))
+    copies = 4 * sum(n - 1 for n in sizes.values())
+    return pl.pallas_call(
+        functools.partial(reduce_kernel, sizes),
+        out_shape=jax.ShapeDtypeStruct(packed.shape, jnp.float32),
+        in_specs=[pl.BlockSpec(memory_space=pltpu.VMEM)],
+        out_specs=pl.BlockSpec(memory_space=pltpu.VMEM),
+        scratch_shapes=[pltpu.VMEM(packed.shape, jnp.float32)]
+        + buffers
+        + [pltpu.SemaphoreType.DMA((copies,)), pltpu.SemaphoreType.DMA((copies,))],
+        compiler_params=pltpu.CompilerParams(collective_id=0, has_side_effects=True),
+        name="reduce_all",
+    )(packed)
+
+
 def factor(packed, breadth, root_scale):
     square = (breadth, breadth)
     return pl.pallas_call(
@@ -178,6 +321,9 @@
             pltpu.VMEM(square, jnp.float32),
             pltpu.VMEM((TILE, breadth), jnp.float32),
         ],
+        cost_estimate=pl.CostEstimate(
+            flops=8 * breadth**3, bytes_accessed=16 * breadth**2, transcendentals=0
+        ),
         name="factor",
     )(packed)
 
@@ -283,11 +429,13 @@
     in_at = carried(jnp.sum(jnp.where(in_match, peer_ids[None, :], 0), axis=1), in_has)
     kind = jnp.where(own_has, 1, jnp.where(in_has, 2, 0)).astype(jnp.int32)
     root_scale = math.sqrt(devices * SLOTS * TILE)
+    sizes = grid_sizes()
+    packed = local_gram(a_rows, lax.dynamic_slice(heights, (group_pos,), (1,)), 2 * devices)
+    packed = reduce_all(packed, sizes)
+    packed, outgoing = lax.optimization_barrier((packed, tile_stack[send_index]))
     received = lax.all_to_all(
-        tile_stack[send_index], "gy", split_axis=0, concat_axis=0, tiled=True
+        outgoing, "gy", split_axis=0, concat_axis=0, tiled=True
     ).reshape(-1, breadth)
-    packed = local_gram(a_rows, lax.dynamic_slice(heights, (group_pos,), (1,)))
-    packed = lax.psum(packed, ("gx", "gy"))
     factor_r, high, low = factor(packed, breadth, root_scale)
     ortho_rows = orthonormal(a_rows, received, own_at, in_at, kind, high, low, root_scale)
     return (ortho_rows, factor_r)

time: 297 us -> 171 us (0.58)
  waiting for transfers between devices: 150 us -> 0.01 us
  Pallas kernels: 110 us -> 150 us
  between operations: 14.1 us -> 0.69 us
    psum x1 -> x0, waiting for transfers between devices: 150 us -> none  [on_device(): packed = lax.psum(packed, ('gx', 'gy'))]
    pallas_call x1 -> x2, Pallas kernels: 11.2 us -> 63.6 us  [the longest x1 53.7 us: reduce_all(): pl.pallas_call(functools.partial(reduce_kernel, sizes), out_shape=jax.Sha...]
    pallas_call x1, Pallas kernels: 80 us -> 67.4 us  [factor(): pl.pallas_call(functools.partial(factor_kernel, root_scale), out_shape=(j...]
  transfers between devices with their start and end apart: 2 -> 1, of which waited for: 1 -> 0; matrix products, arithmetic and copies ran while one was open for 2% -> 2% of each run, Pallas kernels for 31% -> 40%
where the time goes in v2:
time: 171 us; the launch traced here: 170 us
  Pallas kernels  150 us (88%)
  local copies, waits for them, and re-layouts  11.3 us (7%)
  starting transfers between devices  4.56 us (3%)
  other arithmetic  3.46 us (2%)
    pallas_call x1, Pallas kernels, factor(): pl.pallas_call(functools.partial(factor_kernel, root_scale), out_shape=(j...  67.4 us
    pallas_call x1, Pallas kernels, reduce_all(): pl.pallas_call(functools.partial(reduce_kernel, sizes), out_shape=jax.Sha...  53.7 us
    pallas_call x1, Pallas kernels, orthonormal(): pl.pallas_call(functools.partial(ortho_kernel, root_scale), out_shape=jax...  19.2 us
    pallas_call x1, Pallas kernels, local_gram(): pl.pallas_call(gram_kernel, out_shape=jax.ShapeDtypeStruct((packed, 8, TI...  9.94 us
    gather x1, local copies, waits for them, and re-layouts, on_device(): tile_stack[send_index]  6.58 us
    all_to_all x1, starting transfers between devices, on_device(): lax.all_to_all(outgoing, 'gy', split_axis=0, concat_axis=0, tiled=True)  4.56 us
  transfers between devices with their start and end apart: 1, of which 0 were waited for; matrix products, arithmetic and copies ran while one was open for 2% of the time, Pallas kernels for 40%

profile of v2, /device:TPU:0, one launch (start us, length us, event | category | flops | bytes accessed | tf_op | source)
XLA Modules:
  0.0 170.3 jit_solution(4089900841616734940)
XLA Ops:
  0.7 1.2 dynamic_slice.15.height_ref
  1.9 0.9 fusion.9
  2.8 0.8 select_reduce_fusion.7
  3.6 0.1 select_reduce_fusion.5
  3.8 9.9 %gram.1.x_ref = f32[576,8,128]{2,1,0:T(8,128)} custom-call(s32[1]{0:T(128)} %dynamic_slice.15.height_ref, bf16[6144,1024]{1,0:T(8,128)(2,1)} %refs_3_.1), custom_call_target="tpu_custom_call" | custom-call | flops 6442450944 | bytes 12582912 | tf_op jit(solution)/shard_map/gram/pallas_call | solution.py:64
  13.7 53.7 %reduce_all.1.gram_ref = f32[576,8,128]{2,1,0:T(8,128)} custom-call(f32[576,8,128]{2,1,0:T(8,128)} %gram.1.x_ref), custom_call_target="tpu_custom_call" | custom-call | tf_op jit(solution)/shard_map/reduce_all/pallas_call | solution.py:296
  67.4 6.6 %gather_fusion = bf16[8,128,1024]{2,1,0:T(8,128)(2,1)} fusion(bf16[48,128,1024]{2,1,0:T(8,128)(2,1)} %bitcast.14, s32[1024]{0:T(1024)S(1)} %pad_clamp_fusion), kind=kCustom, calls=%fused_computation | custom fusion | bytes 4194336 | tf_op jit(solution)/shard_map/gather | solution.py:435
  74.0 4.6 %all-to-all-start = ((bf16[8,128,1024]{2,1,0:T(8,128)(2,1)}), bf16[8,128,1024]{2,1,0:T(8,128)(2,1)S(1)}, u32[]{:S(2)}, u32[]{:S(2)}) async-start(bf16[8,128,1024]{2,1,0:T(8,128)(2,1)} %gather_fusion), calls=%async_computation | async-start | bytes 4194304 | tf_op jit(solution)/shard_map/all_to_all | solution.py:436
  78.6 0.1 fusion.4
  78.6 0.1 and.104
  78.7 0.1 copy.8
  78.8 0.1 fusion.1
  78.9 0.1 and.95
  79.0 0.1 copy.5
  79.1 0.1 select_reduce_fusion.6
  79.2 0.1 broadcast_in_dim.126
  79.3 0.1 copy.9
  79.4 0.2 select_reduce_fusion.1
  79.6 0.2 select_reduce_fusion
  79.9 0.1 copy.10
  79.9 0.7 reshape.59.in_at
  80.6 0.1 select_reduce_fusion.3
  80.7 0.1 broadcast_in_dim.119
  80.8 0.1 copy.6
  80.9 0.2 select_reduce_fusion.2
  81.1 0.1 copy.7
  81.2 0.6 reshape.58.own_at
  81.8 0.5 select_select_fusion.kind
  82.3 67.4 %factor.1 = (f32[1024,1024]{1,0:T(8,128)}, bf16[1024,1024]{1,0:T(8,128)(2,1)}, bf16[1024,1024]{1,0:T(8,128)(2,1)}) custom-call(f32[576,8,128]{2,1,0:T(8,128)} %reduce_all.1.gram_ref), custom_call_target="tpu_custom_call" | custom-call | flops 8589934592 | bytes 16777216 | tf_op jit(solution)/shard_map/factor/pallas_call | solution.py:311
  149.7 0.0 all-to-all-done
  149.7 1.4 copy-done
  151.1 19.2 %ortho.1 = bf16[4096,1024]{1,0:T(8,128)(2,1)} custom-call(s32[32]{0:T(128)} %reshape.58.own_at, s32[32]{0:T(128)} %reshape.59.in_at, s32[32]{0:T(128)} %select_select_fusion.kind, bf16[6144,1024]{1,0:T(8,128)(2,1)} %refs_3_.1, bf16[6144,1024]{1,0:T(8,128)(2,1)} %refs_3_.1, bf16[6144,1024]{1,0:T(8,128)(2,1)} %refs_3_.1, bf16[6144,1024]{1,0:T(8,128)(2,1)} %refs_3_.1, ...), custom_call_target="tpu_custom_call" | custom-call | tf_op jit(solution)/shard_map/ortho/pallas_call | solution.py:383
  (7 shorter events, 0.1 us)
Async XLA Ops:
  74.0 75.7 %all-to-all-start = ((bf16[8,128,1024]{2,1,0:T(8,128)(2,1)}), bf16[8,128,1024]{2,1,0:T(8,128)(2,1)S(1)}, u32[]{:S(2)}, u32[]{:S(2)}) async-start(bf16[8,128,1024]{2,1,0:T(8,128)(2,1)} %gather_fusion), calls=%async_computation | async-start | bytes 4194304 | tf_op jit(solution)/shard_map/all_to_all | solution.py:436
  149.7 1.4 copy-start

commit v3 on v2

--- a/solution.py
+++ b/solution.py
@@ -14,12 +14,14 @@
 BIG = 256
 PANEL = 8
 REGS = TILE // 8
+STREAMS = 6
 NT = (((1,), (1,)), ((), ()))
-TN = (((0,), (0,)), ((), ()))
-HIGHEST = lax.Precision.HIGHEST
-
-
-def gram_kernel(height_ref, a_ref, out_ref):
+
+
+def gram_kernel(height_ref, sent_at, a_ref, *refs):
+    sent, out_ref, packed_ref = refs[:-2], refs[-2], refs[-1]
+    for g, tile in enumerate(sent):
+        packed_ref[g * TILE : (g + 1) * TILE, :] = tile[...]
     step = pl.program_id(0)
     rows, breadth = a_ref.shape
     live = height_ref[0] * TILE - step * rows
@@ -31,17 +33,13 @@
     def add(block):
         across = block.T
         place = 0
-        for i in range(breadth // BIG):
-            width = (i + 1) * BIG
-            product = lax.dot_general(
-                across[i * BIG : (i + 1) * BIG],
-                block[:, :width],
-                (((1,), (0,)), ((), ())),
-                preferred_element_type=jnp.float32,
+        for i in range(0, breadth, BIG):
+            product = jnp.dot(
+                across[i : i + BIG], block[:, i:], preferred_element_type=jnp.float32
             )
             for top in range(0, BIG, TILE):
-                for j in range((i * BIG + top) // TILE + 1):
-                    piece = product[top : top + TILE, j * TILE : (j + 1) * TILE]
+                for j in range(top, breadth - i, TILE):
+                    piece = product[top : top + TILE, j : j + TILE]
                     out_ref[place : place + REGS] += piece.reshape(REGS, 8, TILE)
                     place += REGS
 
@@ -56,30 +54,49 @@
         add(a_ref[...] * keep)
 
 
-def local_gram(a_rows, height, split):
+def local_gram(a_rows, height, send_index, split):
     total, breadth = a_rows.shape
     rows = GROUP * TILE
     blocks = breadth // TILE
     packed = pl.cdiv(blocks * (blocks + 1) // 2 * REGS, split) * split
+    steps = total // rows
+    peers = send_index.shape[0]
+    each = 1
+    while each * steps < peers or peers % each:
+        each += 1
+    last = peers // each - 1
+
+    def sent_spec(g):
+        return pl.BlockSpec(
+            (TILE, breadth), lambda i, h, t: (t[jnp.minimum(i, last) * each + g], 0)
+        )
+
     return pl.pallas_call(
         gram_kernel,
-        out_shape=jax.ShapeDtypeStruct((packed, 8, TILE), jnp.float32),
+        out_shape=(
+            jax.ShapeDtypeStruct((packed, 8, TILE), jnp.float32),
+            jax.ShapeDtypeStruct((peers * TILE, breadth), a_rows.dtype),
+        ),
         grid_spec=pltpu.PrefetchScalarGridSpec(
-            num_scalar_prefetch=1,
-            grid=(total // rows,),
+            num_scalar_prefetch=2,
+            grid=(steps,),
             in_specs=[
                 pl.BlockSpec(
                     (rows, breadth),
-                    lambda i, h: (jnp.minimum(i, (h[0] - 1) // GROUP), 0),
+                    lambda i, h, t: (jnp.minimum(i, (h[0] - 1) // GROUP), 0),
                 )
-            ],
-            out_specs=pl.BlockSpec((packed, 8, TILE), lambda i, h: (0, 0, 0)),
+            ]
+            + [sent_spec(g) for g in range(each)],
+            out_specs=(
+                pl.BlockSpec((packed, 8, TILE), lambda i, h, t: (0, 0, 0)),
+                pl.BlockSpec((each * TILE, breadth), lambda i, h, t: (jnp.minimum(i, last), 0)),
+            ),
         ),
         cost_estimate=pl.CostEstimate(
             flops=total * breadth * breadth, bytes_accessed=total * breadth * 2, transcendentals=0
         ),
         name="gram",
-    )(height, a_rows)
+    )(height, send_index, a_rows, *([a_rows] * each))
 
 
 def eliminate(block):
@@ -94,35 +111,54 @@
         ]
         for m in range(PANEL):
             at = first + m
-            local = at % 8
+            home, local = at // 8, at % 8
+            skip = home - start
             column = spread[m]
-            pivot = jnp.broadcast_to(column[0][local : local + 1], (8, TILE))
+            pivot = jnp.broadcast_to(column[skip][local : local + 1], (8, TILE))
             inverse = 1.0 / pivot
-            factors = [c * inverse for c in column]
             below = sub > local
+            factors = [c * inverse for c in column[skip:]]
             factors[0] = jnp.where(below, factors[0], 0.0)
             here = lane == at
-            row = jnp.where(here, 1.0, parts[start][local : local + 1])
+            row = jnp.where(here, 1.0, parts[home][local : local + 1])
             row = jnp.broadcast_to(row, (8, TILE))
-            for g in range(start, len(parts)):
-                clear = here & below if g == start else here
-                parts[g] = jnp.where(clear, 0.0, parts[g]) - factors[g - start] * row
             for n in range(m + 1, PANEL):
-                level = jnp.broadcast_to(spread[n][0][local : local + 1], (8, TILE))
-                spread[n] = [c - f * level for c, f in zip(spread[n], factors)]
+                level = jnp.broadcast_to(spread[n][skip][local : local + 1], (8, TILE))
+                spread[n] = spread[n][:skip] + [
+                    c - f * level for c, f in zip(spread[n][skip:], factors)
+                ]
+            for g in range(home, len(parts)):
+                clear = here & below if g == home else here
+                parts[g] = jnp.where(clear, 0.0, parts[g]) - factors[g - home] * row
     return jnp.concatenate(parts, axis=0)
 
 
-def factor_kernel(root_scale, gram_ref, r_ref, high_ref, low_ref, work, line):
+def thirds(value):
+    first = value.astype(jnp.bfloat16)
+    rest = value - first.astype(jnp.float32)
+    second = rest.astype(jnp.bfloat16)
+    third = (rest - second.astype(jnp.float32)).astype(jnp.bfloat16)
+    return first, second, third
+
+
+def left_terms(value):
+    first, second, third = thirds(value)
+    return jnp.concatenate([first, first, second, second, first, third], axis=1)
+
+
+def right_terms(value):
+    first, second, third = thirds(value)
+    return jnp.concatenate([first, second, first, second, third, first], axis=0)
+
+
+def factor_kernel(root_scale, gram_ref, r_ref, high_ref, low_ref, work, line, left, right):
     breadth = r_ref.shape[0]
     count = breadth // TILE
     place = 0
     for i in range(count):
-        for j in range(i + 1):
+        for j in range(i, count):
             block = gram_ref[place : place + REGS].reshape(TILE, TILE)
             work[i * TILE : (i + 1) * TILE, j * TILE : (j + 1) * TILE] = block
-            if j < i:
-                work[j * TILE : (j + 1) * TILE, i * TILE : (i + 1) * TILE] = block.T
             place += REGS
     rows_id = lax.broadcasted_iota(jnp.int32, (TILE, TILE), 0)
     cols_id = lax.broadcasted_iota(jnp.int32, (TILE, TILE), 1)
@@ -131,6 +167,7 @@
     def step(k, carry):
         base = pl.multiple_of(k * TILE, TILE)
         mine = pl.ds(base, TILE)
+        right[...] = right_terms(work[mine, :])
         done = eliminate(work[mine, mine])
         diagonal = jnp.sum(jnp.where(rows_id == cols_id, done, 0.0), axis=1, keepdims=True)
         shrink = 1.0 / jnp.sqrt(diagonal)
@@ -139,7 +176,7 @@
         ) * shrink
         upper = jnp.where(rows_id <= cols_id, done, 0.0) * shrink
         line[...] = jnp.dot(
-            inverse, work[mine, :], precision=HIGHEST, preferred_element_type=jnp.float32
+            left_terms(inverse), right[...], preferred_element_type=jnp.float32
         )
         r_ref[mine, :] = jnp.where(wide_id >= base, line[...], 0.0) * (1.0 / root_scale)
         r_ref[mine, mine] = upper * (1.0 / root_scale)
@@ -149,27 +186,36 @@
         high_ref[mine, :] = high
         low_ref[mine, :] = (solved - high.astype(jnp.float32)).astype(jnp.bfloat16)
 
-        def update(i, carry):
-            theirs = pl.ds(pl.multiple_of(i * TILE, TILE), TILE)
-            left = lax.dot_general(
-                work[theirs, mine], inverse, NT, precision=HIGHEST, preferred_element_type=jnp.float32
-            )
-            work[theirs, mine] = jnp.zeros((TILE, TILE), jnp.float32)
-            work[theirs, :] -= jnp.dot(
-                left, line[...], precision=HIGHEST, preferred_element_type=jnp.float32
-            )
-            return carry
-
-        lax.fori_loop(k + 1, count, update, 0)
+        @pl.when(k + 1 < count)
+        def _():
+            later = jnp.where(wide_id >= base + TILE, line[...], 0.0)
+            left[...] = left_terms(later.T)
+            right[...] = right_terms(line[...])
+
+            def update(i, carry):
+                theirs = pl.ds(pl.multiple_of(i * BIG, BIG), BIG)
+                work[theirs, mine] = jnp.zeros((BIG, TILE), jnp.float32)
+                work[theirs, :] -= jnp.dot(
+                    left[theirs, :], right[...], preferred_element_type=jnp.float32
+                )
+                return carry
+
+            lax.fori_loop((k + 1) * TILE // BIG, breadth // BIG, update, 0)
+
         return carry
 
     lax.fori_loop(0, count, step, 0)
 
 
+def stream_orders():
+    return (("core", "x", "y", "z"), ("core", "y", "x", "z")) * (STREAMS // 2)
+
+
 def reduce_kernel(sizes, x_ref, out_ref, work, *rest):
-    streams = (("core", "x", "y", "z"), ("core", "y", "x", "z"))
+    streams = stream_orders()
+    count = len(streams)
     depth = len(streams[0])
-    arrived, sends, recvs = rest[: 2 * depth], rest[2 * depth], rest[2 * depth + 1]
+    arrived, sends, recvs = rest[: count * depth], rest[count * depth], rest[count * depth + 1]
     at_gx, at_gy = lax.axis_index("gx"), lax.axis_index("gy")
     pair, across = sizes["core"], sizes["x"]
     here = {
@@ -195,7 +241,7 @@
             greeted += 1
     pl.semaphore_wait(barrier, greeted)
 
-    half = x_ref.shape[0] // 2
+    share = x_ref.shape[0] // count
     used = [0]
 
     def send(source, target, where):
@@ -213,9 +259,9 @@
         return copy
 
     pending = []
-    base = [0, half]
-    size = [half, half]
-    bases = [[], []]
+    base = [share * s for s in range(count)]
+    size = [share] * count
+    bases = [[] for _ in range(count)]
 
     def scatter(s, level):
         dim = streams[s][level]
@@ -261,16 +307,17 @@
             copy.wait_recv()
         pending.extend(copies)
 
-    flying = [scatter(s, 0) for s in range(2)]
-    for level in range(depth):
-        for s in range(2):
-            collect(s, level, flying[s])
-            flying[s] = scatter(s, level + 1) if level + 1 < depth else gather(s, level)
-    for level in reversed(range(depth)):
-        for s in range(2):
-            landed(flying[s])
-            if level:
-                flying[s] = gather(s, level - 1)
+    flying = [scatter(s, 0) for s in range(count)]
+    for wave in range(2 * depth + count // 2 - 1):
+        for s in range(count):
+            stage = wave - s // 2
+            if 0 <= stage < depth:
+                collect(s, stage, flying[s])
+                flying[s] = scatter(s, stage + 1) if stage + 1 < depth else gather(s, stage)
+            elif depth <= stage < 2 * depth:
+                landed(flying[s])
+                if stage + 1 < 2 * depth:
+                    flying[s] = gather(s, 2 * depth - 2 - stage)
     for copy in pending:
         copy.wait_send()
 
@@ -285,14 +332,14 @@
 
 
 def reduce_all(packed, sizes):
-    part = packed.shape[0] // 2
+    part = packed.shape[0] // STREAMS
     buffers = []
-    for order in (("core", "x", "y", "z"), ("core", "y", "x", "z")):
+    for order in stream_orders():
         left = part
         for dim in order:
             left //= sizes[dim]
             buffers.append(pltpu.VMEM((max(sizes[dim] - 1, 1), left, 8, TILE), jnp.float32))
-    copies = 4 * sum(n - 1 for n in sizes.values())
+    copies = 2 * STREAMS * sum(n - 1 for n in sizes.values())
     return pl.pallas_call(
         functools.partial(reduce_kernel, sizes),
         out_shape=jax.ShapeDtypeStruct(packed.shape, jnp.float32),
@@ -320,6 +367,8 @@
         scratch_shapes=[
             pltpu.VMEM(square, jnp.float32),
             pltpu.VMEM((TILE, breadth), jnp.float32),
+            pltpu.VMEM((breadth, 6 * TILE), jnp.bfloat16),
+            pltpu.VMEM((6 * TILE, breadth), jnp.bfloat16),
         ],
         cost_estimate=pl.CostEstimate(
             flops=8 * breadth**3, bytes_accessed=16 * breadth**2, transcendentals=0
@@ -403,8 +452,7 @@
     group_pos = lax.axis_index("gy")
     my_index = lax.axis_index("gx") * size_gy + group_pos
     group_base = my_index - group_pos
-    tile_stack = a_rows.reshape(-1, TILE, breadth)
-    stored = tile_stack.shape[0]
+    stored = a_rows.shape[0] // TILE
     tile_ids = jnp.arange(stored, dtype=jnp.int32)
     peer_ids = jnp.arange(size_gy, dtype=jnp.int32)
     slot_ids = jnp.arange(SLOTS, dtype=jnp.int32)
@@ -430,11 +478,12 @@
     kind = jnp.where(own_has, 1, jnp.where(in_has, 2, 0)).astype(jnp.int32)
     root_scale = math.sqrt(devices * SLOTS * TILE)
     sizes = grid_sizes()
-    packed = local_gram(a_rows, lax.dynamic_slice(heights, (group_pos,), (1,)), 2 * devices)
+    height = lax.dynamic_slice(heights, (group_pos,), (1,))
+    packed, outgoing = local_gram(a_rows, height, send_index, STREAMS * devices)
     packed = reduce_all(packed, sizes)
-    packed, outgoing = lax.optimization_barrier((packed, tile_stack[send_index]))
+    packed, outgoing = lax.optimization_barrier((packed, outgoing))
     received = lax.all_to_all(
-        outgoing, "gy", split_axis=0, concat_axis=0, tiled=True
+        outgoing.reshape(-1, TILE, breadth), "gy", split_axis=0, concat_axis=0, tiled=True
     ).reshape(-1, breadth)
     factor_r, high, low = factor(packed, breadth, root_scale)
     ortho_rows = orthonormal(a_rows, received, own_at, in_at, kind, high, low, root_scale)

time: 171 us -> 148 us (0.87)
  Pallas kernels: 150 us -> 133 us
  local copies, waits for them, and re-layouts: 11.3 us -> 4.83 us
    pallas_call x1, Pallas kernels: 67.4 us -> 54.9 us  [factor(): pl.pallas_call(functools.partial(factor_kernel, root_scale), out_shape=(j...]
    gather x1 -> x0, local copies, waits for them, and re-layouts: 6.58 us -> none  [on_device(): tile_stack[send_index]]
    pallas_call x1, Pallas kernels: 53.7 us -> 49 us  [reduce_all(): pl.pallas_call(functools.partial(reduce_kernel, sizes), out_shape=jax.Sha...]
  transfers between devices with their start and end apart: 1 -> 1, of which waited for: 0 -> 0; matrix products, arithmetic and copies ran while one was open for 2% -> 3% of each run, Pallas kernels for 40% -> 37%
where the time goes in v3:
time: 148 us; the launch traced here: 147 us
  Pallas kernels  133 us (90%)
  local copies, waits for them, and re-layouts  4.83 us (3%)
  other arithmetic  3.95 us (3%)
  starting transfers between devices  3.92 us (3%)
    pallas_call x1, Pallas kernels, factor(): pl.pallas_call(functools.partial(factor_kernel, root_scale), out_shape=(j...  54.9 us
    pallas_call x1, Pallas kernels, reduce_all(): pl.pallas_call(functools.partial(reduce_kernel, sizes), out_shape=jax.Sha...  49 us
    pallas_call x1, Pallas kernels, orthonormal(): pl.pallas_call(functools.partial(ortho_kernel, root_scale), out_shape=jax...  19.2 us
    pallas_call x1, Pallas kernels, local_gram(): pl.pallas_call(gram_kernel, out_shape=(jax.ShapeDtypeStruct((packed, 8, T...  10.1 us
    all_to_all x1, starting transfers between devices, on_device(): lax.all_to_all(outgoing.reshape(-1, TILE, breadth), 'gy', split_axis=0, c...  3.92 us
  transfers between devices with their start and end apart: 1, of which 0 were waited for; matrix products, arithmetic and copies ran while one was open for 3% of the time, Pallas kernels for 37%

profile of v3, /device:TPU:0, one launch (start us, length us, event | category | flops | bytes accessed | tf_op | source)
XLA Modules:
  0.0 146.7 jit_solution(9974908044765048271)
XLA Ops:
  0.7 1.3 dynamic_slice.15.height_ref
  2.0 0.9 fusion.8
  2.9 0.8 select_reduce_fusion.7
  3.7 0.6 select_reduce_fusion.5.sent_at
  4.3 10.1 %gram.1 = (f32[576,8,128]{2,1,0:T(8,128)}, bf16[1024,1024]{1,0:T(8,128)(2,1)}) custom-call(s32[1]{0:T(128)} %dynamic_slice.15.height_ref, s32[8]{0:T(128)} %select_reduce_fusion.5.sent_at, bf16[6144,1024]{1,0:T(8,128)(2,1)} %refs_3_.1, bf16[6144,1024]{1,0:T(8,128)(2,1)} %refs_3_.1), custom_call_target="tpu_custom_call" | custom-call | flops 6442450944 | bytes 12582912 | tf_op jit(solution)/shard_map/gram/pallas_call | solution.py:74
  14.4 49.0 %reduce_all.1.gram_ref = f32[576,8,128]{2,1,0:T(8,128)} custom-call(f32[576,8,128]{2,1,0:T(8,128)} %get-tuple-element.9.x_ref), custom_call_target="tpu_custom_call" | custom-call | tf_op jit(solution)/shard_map/reduce_all/pallas_call | solution.py:343
  63.5 3.9 %all-to-all-start = ((bf16[8,128,1024]{2,1,0:T(8,128)(2,1)}), bf16[8,128,1024]{2,1,0:T(8,128)(2,1)S(1)}, u32[]{:S(2)}, u32[]{:S(2)}) async-start(bf16[8,128,1024]{2,1,0:T(8,128)(2,1)} %bitcast.14), calls=%async_computation | async-start | bytes 4194304 | tf_op jit(solution)/shard_map/all_to_all | solution.py:485
  67.4 0.1 fusion.4
  67.5 0.1 and.104
  67.6 0.1 copy.8
  67.7 0.1 fusion.1
  67.8 0.1 and.95
  67.9 0.1 copy.5
  68.0 0.1 select_reduce_fusion.6
  68.1 0.1 broadcast_in_dim.125
  68.2 0.1 copy.9
  68.2 0.2 select_reduce_fusion.1
  68.5 0.2 select_reduce_fusion
  68.7 0.1 copy.10
  68.8 0.7 reshape.46.in_at
  69.4 0.1 select_reduce_fusion.3
  69.6 0.1 broadcast_in_dim.118
  69.6 0.1 copy.6
  69.7 0.2 select_reduce_fusion.2
  70.0 0.1 copy.7
  70.0 0.6 reshape.45.own_at
  70.7 0.5 select_select_fusion.kind
  71.2 54.9 %factor.1 = (f32[1024,1024]{1,0:T(8,128)}, bf16[1024,1024]{1,0:T(8,128)(2,1)}, bf16[1024,1024]{1,0:T(8,128)(2,1)}) custom-call(f32[576,8,128]{2,1,0:T(8,128)} %reduce_all.1.gram_ref), custom_call_target="tpu_custom_call" | custom-call | flops 8589934592 | bytes 16777216 | tf_op jit(solution)/shard_map/factor/pallas_call | solution.py:358
  126.1 0.0 all-to-all-done
  126.1 0.0 copy-start
  126.1 1.4 copy-done
  127.4 19.2 %ortho.1 = bf16[4096,1024]{1,0:T(8,128)(2,1)} custom-call(s32[32]{0:T(128)} %reshape.45.own_at, s32[32]{0:T(128)} %reshape.46.in_at, s32[32]{0:T(128)} %select_select_fusion.kind, bf16[6144,1024]{1,0:T(8,128)(2,1)} %refs_3_.1, bf16[6144,1024]{1,0:T(8,128)(2,1)} %refs_3_.1, bf16[6144,1024]{1,0:T(8,128)(2,1)} %refs_3_.1, bf16[6144,1024]{1,0:T(8,128)(2,1)} %refs_3_.1, ...), custom_call_target="tpu_custom_call" | custom-call | tf_op jit(solution)/shard_map/ortho/pallas_call | solution.py:432
  (4 shorter events, 0.0 us)
Async XLA Ops:
  63.5 62.6 %all-to-all-start = ((bf16[8,128,1024]{2,1,0:T(8,128)(2,1)}), bf16[8,128,1024]{2,1,0:T(8,128)(2,1)S(1)}, u32[]{:S(2)}, u32[]{:S(2)}) async-start(bf16[8,128,1024]{2,1,0:T(8,128)(2,1)} %bitcast.14), calls=%async_computation | async-start | bytes 4194304 | tf_op jit(solution)/shard_map/all_to_all | solution.py:485
  126.1 1.4 copy-start

commit v4 on v3

--- a/solution.py
+++ b/solution.py
@@ -409,13 +409,11 @@
 
 
 def carried(index, used):
-    index = index.reshape(-1, GROUP)
-    used = used.reshape(-1, GROUP)
-    steps = jnp.arange(index.shape[0], dtype=jnp.int32)
-    earlier = used[None, :, :] & (steps[None, :, None] <= steps[:, None, None])
-    last = jnp.max(jnp.where(earlier, steps[None, :, None], -1), axis=1)
-    pick = last[:, None, :] == steps[None, :, None]
-    return jnp.sum(jnp.where(pick, index[None], 0), axis=1).reshape(-1)
+    slots = jnp.arange(index.shape[0], dtype=jnp.int32)
+    lanes = slots % GROUP
+    earlier = used[None, :] & (slots[None, :] <= slots[:, None]) & (lanes[None, :] == lanes[:, None])
+    last = jnp.max(jnp.where(earlier, slots[None, :], -1), axis=1)
+    return jnp.sum(jnp.where(last[:, None] == slots[None, :], index[None, :], 0), axis=1)
 
 
 def orthonormal(a_rows, received, own_at, in_at, kind, high, low, root_scale):

time: 148 us -> 147 us (level)
  local copies, waits for them, and re-layouts: 4.83 us -> 2.68 us
    pallas_call x1, Pallas kernels: 10.1 us -> 11.6 us  [local_gram(): pl.pallas_call(gram_kernel, out_shape=(jax.ShapeDtypeStruct((packed, 8, T...]
  transfers between devices with their start and end apart: 1 -> 1, of which waited for: 0 -> 0; matrix products, arithmetic and copies ran while one was open for 3% -> 2% of each run, Pallas kernels for 37% -> 38%
where the time goes in v4:
time: 147 us; the launch traced here: 146 us
  Pallas kernels  134 us (91%)
  other arithmetic  4.94 us (3%)
  starting transfers between devices  4.18 us (3%)
  local copies, waits for them, and re-layouts  2.68 us (2%)
    pallas_call x1, Pallas kernels, factor(): pl.pallas_call(functools.partial(factor_kernel, root_scale), out_shape=(j...  54.9 us
    pallas_call x1, Pallas kernels, reduce_all(): pl.pallas_call(functools.partial(reduce_kernel, sizes), out_shape=jax.Sha...  48.2 us
    pallas_call x1, Pallas kernels, orthonormal(): pl.pallas_call(functools.partial(ortho_kernel, root_scale), out_shape=jax...  19.2 us
    pallas_call x1, Pallas kernels, local_gram(): pl.pallas_call(gram_kernel, out_shape=(jax.ShapeDtypeStruct((packed, 8, T...  11.6 us
    all_to_all x1, starting transfers between devices, on_device(): lax.all_to_all(outgoing.reshape(-1, TILE, breadth), 'gy', split_axis=0, c...  4.18 us
  transfers between devices with their start and end apart: 1, of which 0 were waited for; matrix products, arithmetic and copies ran while one was open for 2% of the time, Pallas kernels for 38%

profile of v4, /device:TPU:0, one launch (start us, length us, event | category | flops | bytes accessed | tf_op | source)
XLA Modules:
  0.0 146.4 jit_solution(10716325154115410814)
XLA Ops:
  0.7 1.3 dynamic_slice.15.height_ref
  2.0 0.9 fusion.10
  2.9 0.8 select_reduce_fusion.7
  3.7 0.6 select_reduce_fusion.5.sent_at
  4.3 11.6 %gram.1 = (f32[576,8,128]{2,1,0:T(8,128)}, bf16[1024,1024]{1,0:T(8,128)(2,1)}) custom-call(s32[1]{0:T(128)} %dynamic_slice.15.height_ref, s32[8]{0:T(128)} %select_reduce_fusion.5.sent_at, bf16[6144,1024]{1,0:T(8,128)(2,1)} %refs_3_.1, bf16[6144,1024]{1,0:T(8,128)(2,1)} %refs_3_.1), custom_call_target="tpu_custom_call" | custom-call | flops 6442450944 | bytes 12582912 | tf_op jit(solution)/shard_map/gram/pallas_call | solution.py:74
  16.0 48.2 %reduce_all.1.gram_ref = f32[576,8,128]{2,1,0:T(8,128)} custom-call(f32[576,8,128]{2,1,0:T(8,128)} %get-tuple-element.9.x_ref), custom_call_target="tpu_custom_call" | custom-call | tf_op jit(solution)/shard_map/reduce_all/pallas_call | solution.py:343
  64.2 4.2 %all-to-all-start = ((bf16[8,128,1024]{2,1,0:T(8,128)(2,1)}), bf16[8,128,1024]{2,1,0:T(8,128)(2,1)S(1)}, u32[]{:S(2)}, u32[]{:S(2)}) async-start(bf16[8,128,1024]{2,1,0:T(8,128)(2,1)} %bitcast.14), calls=%async_computation | async-start | bytes 4194304 | tf_op jit(solution)/shard_map/all_to_all | solution.py:483
  68.4 0.1 fusion.3
  68.5 0.1 select_reduce_fusion.3
  68.6 0.1 fusion.6
  68.7 0.2 select_reduce_fusion.1
  68.9 0.1 select_reduce_fusion.6
  69.0 0.8 select_reduce_fusion.in_at
  69.8 0.7 select_reduce_fusion.2.own_at
  70.5 0.5 select_select_fusion.kind
  71.0 54.9 %factor.1 = (f32[1024,1024]{1,0:T(8,128)}, bf16[1024,1024]{1,0:T(8,128)(2,1)}, bf16[1024,1024]{1,0:T(8,128)(2,1)}) custom-call(f32[576,8,128]{2,1,0:T(8,128)} %reduce_all.1.gram_ref), custom_call_target="tpu_custom_call" | custom-call | flops 8589934592 | bytes 16777216 | tf_op jit(solution)/shard_map/factor/pallas_call | solution.py:358
  125.9 0.0 all-to-all-done
  125.9 0.0 copy-start
  125.9 1.4 copy-done
  127.3 19.2 %ortho.1 = bf16[4096,1024]{1,0:T(8,128)(2,1)} custom-call(s32[32]{0:T(128)} %select_reduce_fusion.2.own_at, s32[32]{0:T(128)} %select_reduce_fusion.in_at, s32[32]{0:T(128)} %select_select_fusion.kind, bf16[6144,1024]{1,0:T(8,128)(2,1)} %refs_3_.1, bf16[6144,1024]{1,0:T(8,128)(2,1)} %refs_3_.1, bf16[6144,1024]{1,0:T(8,128)(2,1)} %refs_3_.1, ...), custom_call_target="tpu_custom_call" | custom-call | tf_op jit(solution)/shard_map/ortho/pallas_call | solution.py:430
  (4 shorter events, 0.0 us)
Async XLA Ops:
  64.2 61.7 %all-to-all-start = ((bf16[8,128,1024]{2,1,0:T(8,128)(2,1)}), bf16[8,128,1024]{2,1,0:T(8,128)(2,1)S(1)}, u32[]{:S(2)}, u32[]{:S(2)}) async-start(bf16[8,128,1024]{2,1,0:T(8,128)(2,1)} %bitcast.14), calls=%async_computation | async-start | bytes 4194304 | tf_op jit(solution)/shard_map/all_to_all | solution.py:483
  125.9 1.4 copy-start
